TPU v7x, 256 devices: a whole 4x4x8 slice. The times are simulated.
256 devices in a mesh: chan: 8 (over z), tm: 32 (over y, x, core).
Axes of the slice: x: 4, y: 4, z: 8, core: 2. Of those that a mesh axis runs over, the one named last changes fastest.
Arguments:
- symbols: int32 [64, 262144], P('chan', 'tm'), may hold values from 0 to 63
- incidence: int32 [256, 6], P('chan'), may hold values from 0 to 63, as said below
- delays: int32 [256, 6], P('chan'), may hold values from 0 to 63
- gains: float32 [2, 256, 6], P(None, 'chan'), may hold values from -4 to 4
- echoes: bfloat16 [2, 256, 262144], P(None, 'chan', 'tm'), may hold values from -6 to 6
Outputs:
- cancelled: bfloat16 [2, 256, 262144], P(None, 'chan', 'tm')
- weights: float32 [2, 256, 384], P(None, 'chan')
Inputs may be any that keep to these rules, and one draw needn't show every extreme that they name: `incidence`: row r names 6 distinct illuminators, all owned by chan index c = r // 32 or the next index c + 1 taken cyclically: ids from c * 8 to (c + 2) * 8 - 1, modulo 64.
All inputs are finite; a program needn't handle non-finite values.
Results may differ from a plain program's by a relative error of at most 0.024.
Values may be sent and summed in bfloat16 or wider, within the bound.
No kernel may reach another device: no remote copies, remote signals or barrier semaphores. Data moves between devices by JAX's collectives and lax.ppermute only.
A program may use at most 64 MiB of HBM per device.

v0:
```python
import math
import jax
import jax.numpy as jnp
from jax import lax
from jax.sharding import PartitionSpec as P

ACTIVE = 6817
DELAYS = 64
PER_RECV = 6
loading = 0.1
batch_rows = 8
HIGHEST = lax.Precision.HIGHEST


def passed_along(array, axis, by):
    peers = lax.axis_size(axis)
    return lax.ppermute(array, axis, [(i, (i + by) % peers) for i in range(peers)])


def from_behind(block, axis, distance):
    devices = range(lax.axis_size(axis))
    route = [(i - distance, i) for i in devices if i - distance in devices]
    return lax.ppermute(block, axis, route)


def rotation_angle_grid(row_count, col_count, period):
    product = (
        jnp.arange(row_count, dtype=jnp.int32)[:, None]
        * jnp.arange(col_count, dtype=jnp.int32)[None, :]
    )
    phases = (product % period).astype(jnp.float32) * (2.0 * math.pi / period)
    return (jnp.cos(phases), jnp.sin(phases))


def complex_multiply_result(pattern, left_pair, right_pair):
    real_part = jnp.einsum(pattern, left_pair[0], right_pair[0], precision=HIGHEST) - jnp.einsum(
        pattern, left_pair[1], right_pair[1], precision=HIGHEST
    )
    imag_part = jnp.einsum(pattern, left_pair[0], right_pair[1], precision=HIGHEST) + jnp.einsum(
        pattern, left_pair[1], right_pair[0], precision=HIGHEST
    )
    return (real_part, imag_part)


def remodulate(symbols):
    emitter_number, length = symbols.shape
    column_entries = 128
    increment_spacing = length // column_entries
    inphase_amplitude = (2 * (symbols % 8) - 7).astype(jnp.float32) / math.sqrt(42.0)
    quadrature_amplitude = (2 * (symbols // 8) - 7).astype(jnp.float32) / math.sqrt(42.0)
    subcarrier = jnp.arange(length, dtype=jnp.int32) - length // 2
    occupied_tones = (jnp.abs(subcarrier) <= (ACTIVE - 1) // 2).astype(jnp.float32)
    tone_symbols = (
        (inphase_amplitude * occupied_tones).reshape(
            emitter_number, increment_spacing, column_entries
        ),
        (quadrature_amplitude * occupied_tones).reshape(
            emitter_number, increment_spacing, column_entries
        ),
    )
    partial_result = complex_multiply_result(
        "mb,nbd->nmd",
        rotation_angle_grid(increment_spacing, increment_spacing, increment_spacing),
        tone_symbols,
    )
    twiddle = rotation_angle_grid(increment_spacing, column_entries, length)
    partial_result = (
        partial_result[0] * twiddle[0] - partial_result[1] * twiddle[1],
        partial_result[0] * twiddle[1] + partial_result[1] * twiddle[0],
    )
    frequency_spectrum = complex_multiply_result(
        "pho,oj->phj",
        partial_result,
        rotation_angle_grid(column_entries, column_entries, column_entries),
    )
    alternate = (1 - 2 * (jnp.arange(length, dtype=jnp.int32) % 2)).astype(jnp.float32) / math.sqrt(
        ACTIVE
    )
    real_part = (
        jnp.swapaxes(frequency_spectrum[0], 1, 2).reshape(emitter_number, length) * alternate
    )
    imag_part = (
        jnp.swapaxes(frequency_spectrum[1], 1, 2).reshape(emitter_number, length) * alternate
    )
    return jnp.stack([real_part, imag_part], axis=1).astype(jnp.bfloat16)


def lag_table(lag_count):
    spread = jnp.arange(2 * lag_count, dtype=jnp.int32)[:, None, None]
    column = jnp.arange(lag_count, dtype=jnp.int32)[None, :, None]
    lag_pos = jnp.arange(lag_count, dtype=jnp.int32)[None, None, :]
    return (spread == lag_count + column - lag_pos).astype(jnp.float32)


def lag_sums(outer):
    leading = outer.shape[:-2]
    lag_count = outer.shape[-2]
    width = outer.shape[-1]
    flat = outer.reshape(leading + (lag_count * width,))
    flat = jnp.pad(flat, [(0, 0)] * len(leading) + [(0, lag_count)])
    skewed = flat.reshape(leading + (lag_count, width + 1))[..., 1 : lag_count + 1]
    return jnp.flip(jnp.sum(skewed, axis=-2), axis=-1)


def toeplitz_tables(lag_count):
    row_pos = jnp.arange(lag_count, dtype=jnp.int32)[:, None, None]
    col_pos = jnp.arange(lag_count, dtype=jnp.int32)[None, :, None]
    lag_pos = jnp.arange(lag_count, dtype=jnp.int32)[None, None, :]
    lower_part = (row_pos - col_pos == lag_pos).astype(jnp.float32)
    upper_part = ((col_pos - row_pos == lag_pos) & (lag_pos > 0)).astype(jnp.float32)
    return (lower_part, upper_part)


def banded_apply(looked, banded):
    real_part = jnp.einsum(
        "bkqv,bkvp->bqp", looked[:, :, 0], banded[0], preferred_element_type=jnp.float32
    ) - jnp.einsum("bkqv,bkvp->bqp", looked[:, :, 1], banded[1], preferred_element_type=jnp.float32)
    imag_part = jnp.einsum(
        "bkqv,bkvp->bqp", looked[:, :, 0], banded[1], preferred_element_type=jnp.float32
    ) + jnp.einsum("bkqv,bkvp->bqp", looked[:, :, 1], banded[0], preferred_element_type=jnp.float32)
    return (real_part, imag_part)


def local(symbols, incidence, delays, gains, echoes):
    local_refs = remodulate(symbols)
    owned = local_refs.shape[0]
    length = local_refs.shape[2]
    lag_count = DELAYS
    taps_count = PER_RECV * DELAYS
    chan_count = lax.axis_size("chan")
    chan_index = lax.axis_index("chan")
    window_count = 2 * owned
    following = passed_along(local_refs, "chan", -1)
    window = jnp.concatenate([local_refs, following], axis=0)
    previous = from_behind(window[:, :, length - lag_count :], "tm", 1)
    extended = jnp.concatenate([previous, window], axis=2)
    block_count = length // lag_count
    pieces = extended.reshape(window_count, 2, block_count + 1, lag_count)
    frames = jnp.concatenate([pieces[:, :, :-1], pieces[:, :, 1:]], axis=3)
    current = pieces[:, :, 1:]
    tm_count = lax.axis_size("tm")
    tm_index = lax.axis_index("tm")
    scale = 1.0 / (length * tm_count)
    diagonal_table = lag_table(lag_count)
    lag_range = jnp.arange(lag_count, dtype=jnp.int32)

    def pair_row(frame):
        real_part = jnp.einsum(
            "qv,jqp->jpv", frame[0], current[:, 0], preferred_element_type=jnp.float32
        ) + jnp.einsum("qv,jqp->jpv", frame[1], current[:, 1], preferred_element_type=jnp.float32)
        imag_part = jnp.einsum(
            "qv,jqp->jpv", frame[0], current[:, 1], preferred_element_type=jnp.float32
        ) - jnp.einsum("qv,jqp->jpv", frame[1], current[:, 0], preferred_element_type=jnp.float32)
        return jnp.concatenate([lag_sums(real_part), lag_sums(imag_part)], axis=1)

    corr_part = lax.map(pair_row, frames) * scale
    owner_chan = incidence // owned
    slot = (owner_chan - chan_index) % chan_count * owned + incidence % owned
    recv_count = echoes.shape[1]
    group_count = recv_count // batch_rows

    def first_pass(step, carry):
        received_all, cross_all = carry
        start = step * batch_rows
        slots = lax.dynamic_slice_in_dim(slot, start, batch_rows, 0).reshape(-1)
        lag_values = lax.dynamic_slice_in_dim(delays, start, batch_rows, 0)
        gain = lax.dynamic_slice_in_dim(gains, start, batch_rows, 1)
        echo = lax.dynamic_slice_in_dim(echoes, start, batch_rows, 1)
        looked = jnp.take(frames, slots, axis=0).reshape(
            batch_rows, PER_RECV, 2, block_count, 2 * lag_count
        )
        onehot = (lag_values[:, :, None] == lag_range[None, None, :]).astype(jnp.float32)
        gain_taps = gain[:, :, :, None] * onehot[None]
        band = jnp.einsum("vpa,xbka->xbkvp", diagonal_table, gain_taps, precision=HIGHEST)
        band_high = band.astype(jnp.bfloat16)
        band_low = (band - band_high.astype(jnp.float32)).astype(jnp.bfloat16)
        high_re, high_im = banded_apply(looked, band_high)
        low_re, low_im = banded_apply(looked, band_low)
        direct_re = (high_re + low_re).reshape(batch_rows, length)
        direct_im = (high_im + low_im).reshape(batch_rows, length)
        received = jnp.stack(
            [echo[0].astype(jnp.float32) + direct_re, echo[1].astype(jnp.float32) + direct_im]
        ).astype(jnp.bfloat16)
        signal = received.reshape(2, batch_rows, block_count, lag_count)
        real_part = jnp.einsum(
            "bkqv,bqp->bkpv", looked[:, :, 0], signal[0], preferred_element_type=jnp.float32
        ) + jnp.einsum(
            "bkqv,bqp->bkpv", looked[:, :, 1], signal[1], preferred_element_type=jnp.float32
        )
        imag_part = jnp.einsum(
            "bkqv,bqp->bkpv", looked[:, :, 0], signal[1], preferred_element_type=jnp.float32
        ) - jnp.einsum(
            "bkqv,bqp->bkpv", looked[:, :, 1], signal[0], preferred_element_type=jnp.float32
        )
        cross_re = lag_sums(real_part).reshape(batch_rows, taps_count)
        cross_im = lag_sums(imag_part).reshape(batch_rows, taps_count)
        cross_piece = jnp.stack([cross_re, cross_im]) * scale
        received_all = lax.dynamic_update_slice_in_dim(received_all, received, start, 1)
        cross_all = lax.dynamic_update_slice_in_dim(cross_all, cross_piece, start, 1)
        return (received_all, cross_all)

    received_init = jnp.zeros((2, recv_count, length), jnp.bfloat16)
    cross_init = jnp.zeros((2, recv_count, taps_count), jnp.float32)
    received_all, cross_all = lax.fori_loop(0, group_count, first_pass, (received_init, cross_init))
    share = recv_count // tm_count
    corr = lax.psum(corr_part, "tm")
    cross = lax.psum_scatter(cross_all, "tm", scatter_dimension=1, tiled=True)
    mine = lax.dynamic_slice_in_dim(slot, tm_index * share, share, 0)
    selector = (
        mine[:, :, None] == jnp.arange(window_count, dtype=jnp.int32)[None, None, :]
    ).astype(jnp.float32)
    gathered = jnp.einsum("rkw,wvd,rlv->rkld", selector, corr, selector, precision=HIGHEST)
    lower_part, upper_part = toeplitz_tables(lag_count)
    sub_re = gathered[..., :lag_count]
    sub_im = gathered[..., lag_count:]
    gram_re = jnp.einsum("rkld,abd->rkalb", sub_re, lower_part, precision=HIGHEST) + jnp.einsum(
        "rlkd,abd->rkalb", sub_re, upper_part, precision=HIGHEST
    )
    gram_im = jnp.einsum("rkld,abd->rkalb", sub_im, lower_part, precision=HIGHEST) - jnp.einsum(
        "rlkd,abd->rkalb", sub_im, upper_part, precision=HIGHEST
    )
    gram_re = gram_re.reshape(share, taps_count, taps_count) + loading * jnp.eye(
        taps_count, dtype=jnp.float32
    )
    gram_im = gram_im.reshape(share, taps_count, taps_count)
    system = jnp.concatenate(
        [jnp.concatenate([gram_re, -gram_im], axis=2), jnp.concatenate([gram_im, gram_re], axis=2)],
        axis=1,
    )
    factor = jnp.linalg.cholesky(system)
    right_side = jnp.concatenate([cross[0], cross[1]], axis=1)
    solved = jax.vmap(
        lambda chol_factor, vector: jax.scipy.linalg.cho_solve((chol_factor, True), vector)
    )(factor, right_side)
    local_weights = jnp.stack([solved[:, :taps_count], solved[:, taps_count:]])
    weights = lax.all_gather(local_weights, "tm", axis=1, tiled=True)
    taps = weights.astype(jnp.bfloat16).reshape(2, recv_count, PER_RECV, lag_count)
    table_half = diagonal_table.astype(jnp.bfloat16)

    def second_pass(step, cancelled_all):
        start = step * batch_rows
        slots = lax.dynamic_slice_in_dim(slot, start, batch_rows, 0).reshape(-1)
        looked = jnp.take(frames, slots, axis=0).reshape(
            batch_rows, PER_RECV, 2, block_count, 2 * lag_count
        )
        tap_rows = lax.dynamic_slice_in_dim(taps, start, batch_rows, 1)
        banded = jnp.einsum(
            "vpa,xbka->xbkvp", table_half, tap_rows, preferred_element_type=jnp.float32
        ).astype(jnp.bfloat16)
        proj_re, proj_im = banded_apply(looked, banded)
        received = lax.dynamic_slice_in_dim(received_all, start, batch_rows, 1).astype(jnp.float32)
        result = jnp.stack(
            [
                received[0] - proj_re.reshape(batch_rows, length),
                received[1] - proj_im.reshape(batch_rows, length),
            ]
        ).astype(jnp.bfloat16)
        return lax.dynamic_update_slice_in_dim(cancelled_all, result, start, 1)

    cancelled = lax.fori_loop(
        0, group_count, second_pass, jnp.zeros((2, recv_count, length), jnp.bfloat16)
    )
    return (cancelled, weights)


def solution(mesh):
    in_specs = (
        P("chan", "tm"),
        P("chan", None),
        P("chan", None),
        P(None, "chan", None),
        P(None, "chan", "tm"),
    )
    out_specs = (P(None, "chan", "tm"), P(None, "chan", None))
    return jax.shard_map(local, mesh=mesh, in_specs=in_specs, out_specs=out_specs, check_vma=False)
```

profile of v0, /device:TPU:1, one launch (start us, length us, event | category | flops | bytes accessed | tf_op | source)
XLA Modules:
  0.0 828.7 jit_solution(11951167454591355933)
XLA Ops:
  14.2 6.5 collective-permute-start
  34.5 95.9 %while.45 = (s32[]{:T(128)}, f32[16,16,128]{2,0,1:T(8,128)S(1)}, bf16[16,2,128,128]{3,2,1,0:T(8,128)(2,1)S(1)}, bf16[16,2,128,64]{2,3,0,1:T(8,128)(2,1)}, s32[]{:T(128)}, /*index=5*/s32[]{:T(128)}, s32[]{}, f32[]{:T(128)}) while((s32[]{:T(128)}, f32[16,16,128]{2,0,1:T(8,128)S(1)}, bf16[16,2,128,128]{3,2,1,0:T(8,128)(2,1)S(1)}, ...), condition=%wide.region_3.4_spmd, body=%wide.region_0.3_spmd.sunk | while | flops 134610944 | bytes 14368901 | solution.py:156
  132.9 203.9 %while.47 = (s32[]{:T(128)}, bf16[2,32,8192]{2,1,0:T(8,128)(2,1)}, f32[2,32,384]{2,0,1:T(2,128)}, bf16[2,32,8192]{2,1,0:T(8,128)(2,1)}, s32[32,6]{1,0:T(8,128)S(...) while((s32[]{:T(128)}, bf16[2,32,8192]{2,1,0:T(8,128)(2,1)}, ...), condition=%wide.region_20.22_spmd.clone, body=%wide.region_17.21_spmd.clone.sunk | while | flops 1820216704 | bytes 142606928 | solution.py:204
  162.1 5.2 reshape.1090
  213.0 5.2 reshape.1090
  263.9 5.2 reshape.1090
  314.8 5.2 reshape.1090
  337.5 110.9 %all-reduce.9.cloned.1.call-done = (f32[16,16,128]{2,0,1:T(8,128)}, f32[2,32,384]{2,0,1:T(2,128)}) async-done(((f32[16,16,128]{2,0,1:T(8,128)}, f32[2,32,384]{2,0,1:T(2,128)}), (f32[16,16,128]{2,0,1:T(8,128)}, f32[2,32,384]{2,0,1:T(2,128)})) %all-reduce.9.cloned.1.call-update) | async-done | bytes 229392 | tf_op jit(solution)/shard_map/psum | solution.py:206
  464.8 5.4 bitcast_add_fusion.1
  483.8 11.7 %custom-call.56 = f32[1,128,128]{2,1,0:T(8,128)S(1)} custom-call(f32[1,128,128]{2,1,0:T(8,128)S(1)} %cholesky.427), custom_call_target="Cholesky" | custom-call | tf_op jit(solution)/shard_map/jit(cholesky)/cholesky | solution.py:230
  496.3 10.6 %custom-call.57 = f32[1,1,128,128]{2,3,1,0:T(8,128)S(1)} custom-call(f32[1,1,128,128]{3,2,1,0:T(8,128)} %get-tuple-element.625), custom_call_target="InvertDiagBlocksLowerTriangular" | custom-call | tf_op jit(solution)/shard_map/jit(cholesky)/cholesky | solution.py:230
  510.5 12.3 %custom-call.58 = f32[1,128,128]{2,1,0:T(8,128)} custom-call(f32[1,128,128]{2,1,0:T(8,128)S(1)} %cholesky.431), custom_call_target="Cholesky" | custom-call | tf_op jit(solution)/shard_map/jit(cholesky)/cholesky | solution.py:230
  525.0 10.6 %custom-call.59 = f32[1,1,128,128]{2,3,1,0:T(8,128)} custom-call(f32[1,1,128,128]{3,2,1,0:T(8,128)S(1)} %get-tuple-element.622), custom_call_target="InvertDiagBlocksLowerTriangular" | custom-call | tf_op jit(solution)/shard_map/jit(cholesky)/cholesky | solution.py:230
  539.2 12.3 %custom-call.60 = f32[1,128,128]{2,1,0:T(8,128)} custom-call(f32[1,128,128]{2,1,0:T(8,128)S(1)} %cholesky.436), custom_call_target="Cholesky" | custom-call | tf_op jit(solution)/shard_map/jit(cholesky)/cholesky | solution.py:230
  553.1 10.4 %custom-call.61 = f32[1,1,128,128]{2,3,1,0:T(8,128)} custom-call(f32[1,1,128,128]{3,2,1,0:T(8,128)S(1)} %get-tuple-element.619), custom_call_target="InvertDiagBlocksLowerTriangular" | custom-call | tf_op jit(solution)/shard_map/jit(cholesky)/cholesky | solution.py:230
  567.0 12.5 %custom-call.62 = f32[1,128,128]{2,1,0:T(8,128)} custom-call(f32[1,128,128]{2,1,0:T(8,128)S(1)} %cholesky.441), custom_call_target="Cholesky" | custom-call | tf_op jit(solution)/shard_map/jit(cholesky)/cholesky | solution.py:230
  581.1 10.4 %custom-call.63 = f32[1,1,128,128]{2,3,1,0:T(8,128)} custom-call(f32[1,1,128,128]{3,2,1,0:T(8,128)S(1)} %get-tuple-element.616), custom_call_target="InvertDiagBlocksLowerTriangular" | custom-call | tf_op jit(solution)/shard_map/jit(cholesky)/cholesky | solution.py:230
  594.9 12.3 %custom-call.64 = f32[1,128,128]{2,1,0:T(8,128)} custom-call(f32[1,128,128]{2,1,0:T(8,128)S(1)} %cholesky.446), custom_call_target="Cholesky" | custom-call | tf_op jit(solution)/shard_map/jit(cholesky)/cholesky | solution.py:230
  608.8 10.4 %custom-call.65 = f32[1,1,128,128]{2,3,1,0:T(8,128)} custom-call(f32[1,1,128,128]{3,2,1,0:T(8,128)S(1)} %get-tuple-element.613), custom_call_target="InvertDiagBlocksLowerTriangular" | custom-call | tf_op jit(solution)/shard_map/jit(cholesky)/cholesky | solution.py:230
  621.6 12.7 %custom-call.66 = f32[1,128,128]{2,1,0:T(8,128)} custom-call(f32[1,128,128]{2,1,0:T(8,128)S(1)} %fusion.93), custom_call_target="Cholesky" | custom-call | tf_op jit(solution)/shard_map/jit(cholesky)/cholesky | solution.py:230
  641.3 21.0 %while.46 = (s32[]{:T(128)}, f32[1,768,768]{2,1,0:T(8,128)}, s32[6,2]{0,1:T(2,128)S(1)}, f32[6,1,128,128]{3,2,1,0:T(8,128)}, s32[]{:T(128)}) while((s32[]{:T(128)}, f32[1,768,768]{2,1,0:T(8,128)}, s32[6,2]{0,1:T(2,128)S(1)}, f32[6,1,128,128]{3,2,1,0:T(8,128)}, s32[]{:T(128)}) %tuple.166), condition=%wide.while_cond, body=%wide.while_body.sunk | while | flops 2 | bytes 132705 | solution.py:233
  662.3 59.8 %custom-call.67 = f32[1,6,128,128]{2,3,1,0:T(8,128)S(1)} custom-call(f32[1,6,128,128]{3,2,1,0:T(8,128)} %bitcast.868), custom_call_target="InvertDiagBlocksLowerTriangular" | custom-call | tf_op jit(solution)/shard_map/vmap(jit(_cho_solve))/triangular_solve | solution.py:233
  737.8 23.6 %all_gather.3 = f32[2,32,384]{2,0,1:T(2,128)S(1)} all-gather(f32[2,1,384]{2,0,1:T(2,128)S(1)} %pad_maximum_fusion.5), channel_id=1, replica_groups=mesh['chan'=8,'tm'=32] {'tm'}, dimensions={1}, use_global_device_ids=true | all-gather | bytes 101376 | tf_op jit(solution)/shard_map/all_gather | solution.py:236
  763.9 57.8 %while.48 = (s32[]{:T(128)}, bf16[2,32,8192]{2,1,0:T(8,128)(2,1)}, bf16[2,32,8192]{2,1,0:T(8,128)(2,1)}, s32[32,6]{1,0:T(8,128)S(1)}, bf16[16,2,128,128]{3,2,1,0...) while((s32[]{:T(128)}, bf16[2,32,8192]{2,1,0:T(8,128)(2,1)}, ...), condition=%wide.region_23.25_spmd.clone, body=%wide.region_22.24_spmd.clone.sunk | while | flops 508298688 | bytes 64534532 | solution.py:260
  (824 shorter events, 452.6 us)
Async XLA Ops:
  7.2 441.2 %all-reduce.9.cloned.1.call-start = ((), (), s32[]{:S(2)}) async-start(), calls=%async_computation | async-start | bytes 458752 | tf_op jit(solution)/shard_map/psum | solution.py:206
  12.9 8.4 %copy-start.17 = (s32[32,6]{0,1:T(8,128)S(1)}, s32[32,6]{0,1:T(8,128)}, u32[]{:S(2)}) copy-start(s32[32,6]{0,1:T(8,128)} %param.14) | copy-start | bytes 2308
  14.2 11.4 %collective-permute-start = (bf16[8,2,8192]{2,0,1:T(8,128)(2,1)S(1)}, bf16[8,2,8192]{2,0,1:T(8,128)(2,1)S(1)}, u32[]{:S(2)}, u32[]{:S(2)}) collective-permute-start(bf16[8,2,8192]{2,0,1:T(8,128)(2,1)S(1)} %pad_maximum_fusion.2), channel_id=1, source_target_pairs={{0,224},{32,0},{64,32},{96,64},{128,96},{160,128},{192,160},{224,1... | collective-permute-start | bytes 786440 | tf_op jit(solution)/shard_map/ppermute | solution.py:17
  25.7 5.6 collective-permute-start.1
  34.5 98.4 %copy-start.15 = (f32[2,32,6]{1,0,2:T(2,128)S(1)}, f32[2,32,6]{1,0,2:T(2,128)}, u32[]{:S(2)}) copy-start(f32[2,32,6]{1,0,2:T(2,128)} %param.16) | copy-start | bytes 4612
  34.5 98.3 %copy-start.16 = (s32[32,6]{0,1:T(8,128)S(1)}, s32[32,6]{0,1:T(8,128)}, u32[]{:S(2)}) copy-start(s32[32,6]{0,1:T(8,128)} %param.15) | copy-start | bytes 2308
  132.9 204.0 %copy-start.19 = (u32[256]{0:T(256)S(1)}, u32[256]{0:T(256)}, u32[]{:S(2)}) copy-start(u32[256]{0:T(256)} %constant.562) | copy-start | bytes 3076
  132.9 316.9 %copy-start.14 = (s32[64,64]{1,0:T(8,128)S(1)}, s32[64,64]{1,0:T(8,128)}, u32[]{:S(2)}) copy-start(s32[64,64]{1,0:T(8,128)} %iota_subtract_fusion.1) | copy-start | bytes 49156
  138.2 5.5 copy-start.5
  143.7 3.0 copy-start
  147.8 2.6 copy-start.1
  189.1 5.5 copy-start.5
  194.5 3.0 copy-start
  198.7 2.6 copy-start.1
  240.0 5.5 copy-start.5
  245.4 3.0 copy-start
  290.8 5.5 copy-start.5
  296.3 3.0 copy-start
  336.8 120.4 %copy-start.18 = (pred[64]{0:T(512)(128)(4,1)S(1)}, pred[64]{0:T(512)(128)(4,1)}, u32[]{:S(2)}) copy-start(pred[64]{0:T(512)(128)(4,1)} %iota_compare_fusion.11) | copy-start | bytes 196
  463.9 10.7 %copy-start.7 = (f32[1,384,384]{1,2,0:T(8,128)}, f32[1,384,384]{1,2,0:T(8,128)S(1)}, u32[]{:S(2)}) copy-start(f32[1,384,384]{1,2,0:T(8,128)S(1)} %reshape.1060) | copy-start | bytes 1769476
  769.6 2.7 copy-start.3
  784.0 2.7 copy-start.3
  798.4 2.7 copy-start.3
  812.8 2.7 copy-start.3
  (21 other events, 37.5 us)
Sparse Core Ops, SparseCore 0:
  336.9 111.3 all-reduce.8
where the time goes:
time: 838 us; the launch traced here: 829 us
  other arithmetic  266 us (32%)
  local copies, waits for them, and re-layouts  230 us (27%)
  matrix products  160 us (19%)
  waiting for transfers between devices  114 us (14%)
  blocking collectives  23.6 us (3%)
  between operations  18.6 us (2%)
  starting transfers between devices  11.6 us (1%)
    another operation x23, other arithmetic, local(): factor = jnp.linalg.cholesky(system)  136 us
    psum x1, waiting for transfers between devices, local(): corr = lax.psum(corr_part, 'tm')  111 us
    reshape x40, local copies, waits for them, and re-layouts, lag_sums(): flat.reshape(leading + (lag_count, width + 1))[..., 1:lag_count + 1]  81.1 us
    another operation x3, other arithmetic, local(): jax.scipy.linalg.cho_solve((chol_factor, True), vector)  61.9 us
    all_gather x1, blocking collectives, local(): weights = lax.all_gather(local_weights, 'tm', axis=1, tiled=True)  23.6 us
    another operation x21, local copies, waits for them, and re-layouts  23.2 us
    reduce_sum x40, other arithmetic, lag_sums(): return jnp.flip(jnp.sum(skewed, axis=-2), axis=-1)  22 us
    dot_general x12, matrix products, banded_apply(): jnp.einsum('bkqv,bkvp->bqp', looked[:, :, 1], banded[1], preferred_elemen...  21 us
  transfers between devices with their start and end apart: 3, of which 2 were waited for; matrix products, arithmetic and copies ran while one was open for 0% of the time, Pallas kernels for 0%

commit v1 on v0

--- a/solution.py
+++ b/solution.py
@@ -203,7 +203,7 @@
     cross_init = jnp.zeros((2, recv_count, taps_count), jnp.float32)
     received_all, cross_all = lax.fori_loop(0, group_count, first_pass, (received_init, cross_init))
     share = recv_count // tm_count
-    corr = lax.psum(corr_part, "tm")
+    corr = jnp.sum(lax.all_gather(corr_part, "tm"), axis=0)
     cross = lax.psum_scatter(cross_all, "tm", scatter_dimension=1, tiled=True)
     mine = lax.dynamic_slice_in_dim(slot, tm_index * share, share, 0)
     selector = (

time: 838 us -> 877 us (1.047)
  waiting for transfers between devices: 114 us -> 164 us
  matrix products: 160 us -> 128 us
  local copies, waits for them, and re-layouts: 230 us -> 247 us
    psum x1 -> x0, waiting for transfers between devices: 111 us -> none  [local(): corr = lax.psum(corr_part, 'tm')]
    unnamed x1 -> x3, waiting for transfers between devices: 0.02 us -> 107 us
    all_gather x0 -> x1, waiting for transfers between devices: none -> 52.5 us  [local(): corr = jnp.sum(lax.all_gather(corr_part, 'tm'), axis=0)]
    dot_general x12, matrix products: 21 us -> 7.76 us  [banded_apply(): jnp.einsum('bkqv,bkvp->bqp', looked[:, :, 1], banded[1], preferred_elemen...]
  transfers between devices with their start and end apart: 3 -> 4, of which waited for: 2 -> 4; matrix products, arithmetic and copies ran while one was open for 0% -> 1% of each run, Pallas kernels for 0% -> 0%
where the time goes in v1:
time: 877 us; the launch traced here: 868 us
  other arithmetic  271 us (31%)
  local copies, waits for them, and re-layouts  247 us (28%)
  waiting for transfers between devices  164 us (19%)
  matrix products  128 us (15%)
  blocking collectives  24 us (3%)
  between operations  18.7 us (2%)
  starting transfers between devices  11.6 us (1%)
    another operation x23, other arithmetic, local(): factor = jnp.linalg.cholesky(system)  136 us
    unnamed x3, waiting for transfers between devices  107 us
    reshape x40, local copies, waits for them, and re-layouts, lag_sums(): flat.reshape(leading + (lag_count, width + 1))[..., 1:lag_count + 1]  85.5 us
    another operation x3, other arithmetic, local(): jax.scipy.linalg.cho_solve((chol_factor, True), vector)  61.4 us
    all_gather x1, waiting for transfers between devices, local(): corr = jnp.sum(lax.all_gather(corr_part, 'tm'), axis=0)  52.5 us
    all_gather x1, blocking collectives, local(): weights = lax.all_gather(local_weights, 'tm', axis=1, tiled=True)  24 us
    another operation x21, local copies, waits for them, and re-layouts  23.2 us
    reduce_sum x40, other arithmetic, lag_sums(): return jnp.flip(jnp.sum(skewed, axis=-2), axis=-1)  22 us
  transfers between devices with their start and end apart: 4, of which 4 were waited for; matrix products, arithmetic and copies ran while one was open for 1% of the time, Pallas kernels for 0%

profile of v1, /device:TPU:1, one launch (start us, length us, event | category | flops | bytes accessed | tf_op | source)
XLA Modules:
  0.0 868.4 jit_solution(7287134889880938872)
XLA Ops:
  14.2 6.5 collective-permute-start
  34.2 95.0 %while.45 = (s32[]{:T(128)}, f32[16,16,128]{2,1,0:T(8,128)S(1)}, bf16[16,2,128,128]{3,2,1,0:T(8,128)(2,1)S(1)}, bf16[16,2,128,64]{2,3,0,1:T(8,128)(2,1)}, s32[]{:T(128)}, /*index=5*/s32[]{:T(128)}, s32[]{}, f32[]{:T(128)}) while((s32[]{:T(128)}, f32[16,16,128]{2,1,0:T(8,128)S(1)}, bf16[16,2,128,128]{3,2,1,0:T(8,128)(2,1)S(1)}, ...), condition=%wide.region_3.4_spmd, body=%wide.region_0.3_spmd.sunk | while | flops 134610944 | bytes 14360717 | solution.py:156
  130.4 203.5 %while.47 = (s32[]{:T(128)}, bf16[2,32,8192]{2,1,0:T(8,128)(2,1)}, f32[2,32,384]{2,0,1:T(2,128)S(1)}, bf16[2,32,8192]{2,1,0:T(8,128)(2,1)}, s32[32,6]{1,0:T(8,12...) while((s32[]{:T(128)}, bf16[2,32,8192]{2,1,0:T(8,128)(2,1)}, ...), condition=%wide.region_20.22_spmd.clone, body=%wide.region_17.21_spmd.clone.sunk | while | flops 1820216704 | bytes 139732624 | solution.py:204
  165.6 6.3 reshape.1088
  216.4 6.3 reshape.1088
  267.2 6.3 reshape.1088
  317.9 6.3 reshape.1088
  337.6 106.5 %all-reduce.8.cloned.1.call-done = f32[2,32,384]{2,0,1:T(2,128)} async-done(((f32[2,32,384]{2,0,1:T(2,128)}), f32[2,32,384]{2,0,1:T(2,128)}) %all-reduce.8.cloned.1.call-update) | async-done | bytes 98320
  445.5 52.5 %all-gather.3.cloned.1.call-done = f32[512,16,128]{2,1,0:T(8,128)} async-done(((f32[16,16,128]{2,1,0:T(8,128)}), f32[512,16,128]{2,1,0:T(8,128)}) %all-gather.3.cloned.1.call-update) | async-done | bytes 4194320 | tf_op jit(solution)/shard_map/all_gather | solution.py:206
  534.2 11.7 %custom-call.56 = f32[1,128,128]{2,1,0:T(8,128)S(1)} custom-call(f32[1,128,128]{2,1,0:T(8,128)S(1)} %cholesky.427), custom_call_target="Cholesky" | custom-call | tf_op jit(solution)/shard_map/jit(cholesky)/cholesky | solution.py:230
  547.4 10.6 %custom-call.57 = f32[1,1,128,128]{2,3,1,0:T(8,128)S(1)} custom-call(f32[1,1,128,128]{3,2,1,0:T(8,128)} %get-tuple-element.645), custom_call_target="InvertDiagBlocksLowerTriangular" | custom-call | tf_op jit(solution)/shard_map/jit(cholesky)/cholesky | solution.py:230
  562.2 12.5 %custom-call.58 = f32[1,128,128]{2,1,0:T(8,128)S(1)} custom-call(f32[1,128,128]{2,1,0:T(8,128)} %cholesky.431), custom_call_target="Cholesky" | custom-call | tf_op jit(solution)/shard_map/jit(cholesky)/cholesky | solution.py:230
  576.0 10.8 %custom-call.59 = f32[1,1,128,128]{2,3,1,0:T(8,128)S(1)} custom-call(f32[1,1,128,128]{3,2,1,0:T(8,128)} %get-tuple-element.642), custom_call_target="InvertDiagBlocksLowerTriangular" | custom-call | tf_op jit(solution)/shard_map/jit(cholesky)/cholesky | solution.py:230
  590.4 12.3 %custom-call.60 = f32[1,128,128]{2,1,0:T(8,128)} custom-call(f32[1,128,128]{2,1,0:T(8,128)S(1)} %cholesky.436), custom_call_target="Cholesky" | custom-call | tf_op jit(solution)/shard_map/jit(cholesky)/cholesky | solution.py:230
  604.3 10.4 %custom-call.61 = f32[1,1,128,128]{2,3,1,0:T(8,128)} custom-call(f32[1,1,128,128]{3,2,1,0:T(8,128)S(1)} %get-tuple-element.639), custom_call_target="InvertDiagBlocksLowerTriangular" | custom-call | tf_op jit(solution)/shard_map/jit(cholesky)/cholesky | solution.py:230
  618.3 12.5 %custom-call.62 = f32[1,128,128]{2,1,0:T(8,128)} custom-call(f32[1,128,128]{2,1,0:T(8,128)S(1)} %cholesky.441), custom_call_target="Cholesky" | custom-call | tf_op jit(solution)/shard_map/jit(cholesky)/cholesky | solution.py:230
  632.3 10.4 %custom-call.63 = f32[1,1,128,128]{2,3,1,0:T(8,128)} custom-call(f32[1,1,128,128]{3,2,1,0:T(8,128)S(1)} %get-tuple-element.636), custom_call_target="InvertDiagBlocksLowerTriangular" | custom-call | tf_op jit(solution)/shard_map/jit(cholesky)/cholesky | solution.py:230
  646.1 12.3 %custom-call.64 = f32[1,128,128]{2,1,0:T(8,128)} custom-call(f32[1,128,128]{2,1,0:T(8,128)S(1)} %cholesky.446), custom_call_target="Cholesky" | custom-call | tf_op jit(solution)/shard_map/jit(cholesky)/cholesky | solution.py:230
  660.0 10.4 %custom-call.65 = f32[1,1,128,128]{2,3,1,0:T(8,128)} custom-call(f32[1,1,128,128]{3,2,1,0:T(8,128)S(1)} %get-tuple-element.633), custom_call_target="InvertDiagBlocksLowerTriangular" | custom-call | tf_op jit(solution)/shard_map/jit(cholesky)/cholesky | solution.py:230
  672.8 12.7 %custom-call.66 = f32[1,128,128]{2,1,0:T(8,128)} custom-call(f32[1,128,128]{2,1,0:T(8,128)S(1)} %fusion.94), custom_call_target="Cholesky" | custom-call | tf_op jit(solution)/shard_map/jit(cholesky)/cholesky | solution.py:230
  692.5 21.0 %while.46 = (s32[]{:T(128)}, f32[1,768,768]{2,1,0:T(8,128)}, s32[6,2]{0,1:T(2,128)S(1)}, f32[6,1,128,128]{3,2,1,0:T(8,128)}, s32[]{:T(128)}) while((s32[]{:T(128)}, f32[1,768,768]{2,1,0:T(8,128)}, s32[6,2]{0,1:T(2,128)S(1)}, f32[6,1,128,128]{3,2,1,0:T(8,128)}, s32[]{:T(128)}) %tuple.170), condition=%wide.while_cond, body=%wide.while_body.sunk | while | flops 2 | bytes 132205 | solution.py:233
  713.5 59.8 %custom-call.67 = f32[1,6,128,128]{2,3,1,0:T(8,128)S(1)} custom-call(f32[1,6,128,128]{3,2,1,0:T(8,128)} %bitcast.869), custom_call_target="InvertDiagBlocksLowerTriangular" | custom-call | tf_op jit(solution)/shard_map/vmap(jit(_cho_solve))/triangular_solve | solution.py:233
  787.7 24.0 %all_gather.11 = f32[2,32,384]{2,0,1:T(2,128)S(1)} all-gather(f32[2,1,384]{2,0,1:T(2,128)S(1)} %pad_maximum_fusion.4), channel_id=1, replica_groups=mesh['chan'=8,'tm'=32] {'tm'}, dimensions={1}, use_global_device_ids=true | all-gather | bytes 101376 | tf_op jit(solution)/shard_map/all_gather | solution.py:236
  813.6 47.8 %while.48 = (s32[]{:T(128)}, bf16[2,32,8192]{2,1,0:T(8,128)(2,1)}, bf16[2,32,8192]{2,1,0:T(8,128)(2,1)}, s32[32,6]{1,0:T(8,128)S(1)}, bf16[16,2,128,128]{3,2,1,0...) while((s32[]{:T(128)}, bf16[2,32,8192]{2,1,0:T(8,128)(2,1)}, ...), condition=%wide.region_23.25_spmd.clone, body=%wide.region_22.24_spmd.clone.sunk | while | flops 508298688 | bytes 39385036 | solution.py:260
  (800 shorter events, 444.4 us)
Async XLA Ops:
  7.2 437.0 %all-reduce.8.cloned.1.call-start = ((), (), s32[]{:S(2)}) async-start(), calls=%async_computation.1 | async-start | bytes 196608
  12.9 7.8 copy-start.17
  14.2 11.5 %collective-permute-start = (bf16[8,2,8192]{2,0,1:T(8,128)(2,1)S(1)}, bf16[8,2,8192]{2,0,1:T(8,128)(2,1)S(1)}, u32[]{:S(2)}, u32[]{:S(2)}) collective-permute-start(bf16[8,2,8192]{2,0,1:T(8,128)(2,1)S(1)} %pad_maximum_fusion.1), channel_id=1, source_target_pairs={{0,224},{32,0},{64,32},{96,64},{128,96},{160,128},{192,160},{224,1... | collective-permute-start | bytes 786440 | tf_op jit(solution)/shard_map/ppermute | solution.py:17
  25.7 5.3 collective-permute-start.1
  34.2 96.2 %copy-start.12 = (f32[2,32,6]{1,0,2:T(2,128)S(1)}, f32[2,32,6]{1,0,2:T(2,128)}, u32[]{:S(2)}) copy-start(f32[2,32,6]{1,0,2:T(2,128)} %param.16) | copy-start | bytes 4612
  34.2 96.2 %copy-start.15 = (s32[32,6]{0,1:T(8,128)S(1)}, s32[32,6]{0,1:T(8,128)}, u32[]{:S(2)}) copy-start(s32[32,6]{0,1:T(8,128)} %param.15) | copy-start | bytes 2308
  142.4 5.5 copy-start
  150.9 2.9 copy-start.1
  174.0 7.3 copy-start.13
  174.0 7.3 copy-start.16
  193.1 5.5 copy-start
  201.7 2.9 copy-start.1
  224.8 7.3 copy-start.13
  224.8 7.3 copy-start.16
  243.9 5.5 copy-start
  252.4 2.9 copy-start.1
  257.3 2.4 copy-start.2
  275.6 7.3 copy-start.13
  275.6 7.3 copy-start.16
  294.7 5.5 copy-start
  303.2 2.9 copy-start.1
  326.3 7.3 copy-start.13
  326.3 7.3 copy-start.16
  334.6 163.5 %all-gather.3.cloned.1.call-start = ((), (), s32[]{:S(2)}) async-start(), calls=%async_computation | async-start | bytes 4325376 | tf_op jit(solution)/shard_map/all_gather | solution.py:206
  (16 other events, 21.0 us)
Sparse Core Ops, SparseCore 0:
  334.7 109.3 all-reduce.7
  447.2 50.7 all-gather.2
